TPU v7x, 32 devices: a whole 2x2x4 slice. The times are simulated.
32 devices in a mesh: groups: 2 (over x), wide: 16 (over z, y, core).
Axes of the slice: x: 2, y: 2, z: 4, core: 2. Of those that a mesh axis runs over, the one named last changes fastest.
Arguments:
- hidden_states: bfloat16 [2048, 64, 1024], P(('groups', 'wide')), parts along dimension 0, may hold values from -6 to 6
- block_owner: int32 [2048, 1], P(('groups', 'wide')), parts along dimension 0, may hold values from 0 to 15; in each aligned block of 64 rows (0 to 63, 64 to 127, ...) at most 8 rows name the same one
- token_doc: int32 [2048, 64], P(('groups', 'wide')), parts along dimension 0, may hold values from 0 to 7, never falling along the last dimension, each value on 1 to 32 neighbouring positions
- token_live: int32 [2048, 64], P(('groups', 'wide')), parts along dimension 0, may hold values 0 or 1
- proj_weight: bfloat16 [1024, 128], replicated, may hold values from -0.1875 to 0.1875
- queries: bfloat16 [2048, 128], P(('groups', 'wide')), parts along dimension 0, may hold values from -1.5 to 1.5
Outputs:
- scores: float32 [256, 1024], P(('groups', 'wide')), parts along dimension 0
There are 2 independent parts, one for each index of `groups`. A program takes and returns all parts, laid end to end along the dimension named above; an argument that names none is the same for every part. Nothing has to cross between parts.
Inputs may be any that keep to these rules, and one draw needn't show every extreme that they name: `block_owner`: among the 64 blocks of one index of wide no owner is named by more than 8 blocks, a bound that some block reaches. `token_doc`: within a block the ids never fall and every id appears.
All inputs are finite; a program needn't handle non-finite values. No bound on the sum of `token_live` on one device may be relied on, other than what follows from the above.
Results may differ from a plain program's by a relative error of at most 0.0011.
Values may be sent and summed in bfloat16 or wider, within the bound.
No kernel may reach another device: no remote copies, remote signals or barrier semaphores. Data moves between devices by JAX's collectives and lax.ppermute only.
A program may use at most 64 MiB of HBM per device.

v0:
```python
import jax
import jax.numpy as jnp
from jax import lax
from jax.sharding import PartitionSpec as P

DOC_DEV = 8


def finish(highest):
    return jnp.where(highest > -100000000.0, highest, jnp.float32(0.0))


def slot_sources(block_owner, owner_count, capacity):
    nblocks = block_owner.shape[0]
    owners = block_owner[:, 0]
    onehot = (owners[:, None] == jnp.arange(owner_count, dtype=jnp.int32)[None, :]).astype(
        jnp.int32
    )
    earlier = jnp.cumsum(onehot, axis=0) - onehot
    rank_in = jnp.sum(earlier * onehot, axis=1)
    slot_of = owners * capacity + rank_in
    matches = slot_of[None, :] == jnp.arange(owner_count * capacity, dtype=jnp.int32)[:, None]
    picked = (
        jnp.sum(
            matches.astype(jnp.int32) * (jnp.arange(nblocks, dtype=jnp.int32)[None, :] + 1), axis=1
        )
        - 1
    )
    return jnp.where(picked < 0, nblocks, picked)


def local(hidden_states, block_owner, token_doc, token_live, proj_weight, queries):
    nblocks, block_len, model_width = hidden_states.shape
    owner_count = lax.axis_size("wide")
    capacity = max(2, (2 * nblocks + owner_count - 1) // owner_count)
    projected = jnp.dot(
        hidden_states.reshape(nblocks * block_len, model_width),
        proj_weight,
        preferred_element_type=jnp.float32,
    )
    vectors = (
        projected * lax.rsqrt(jnp.sum(projected * projected, axis=1, keepdims=True) + 1e-06)
    ).astype(jnp.bfloat16)
    doc_code = jnp.where(token_live == 1, token_doc, -1)
    source = slot_sources(block_owner, owner_count, capacity)
    query_piece = lax.all_gather(queries, "wide", axis=0, tiled=True)
    rows = query_piece.shape[0]
    similar = jnp.dot(query_piece, vectors.T, preferred_element_type=jnp.float32).reshape(
        rows, nblocks, block_len
    )
    partial_value = jnp.stack(
        [
            jnp.max(jnp.where(doc_code[None, :, :] == doc_slot, similar, -1000000000.0), axis=2)
            for doc_slot in range(DOC_DEV)
        ]
    )
    partial_value = jnp.transpose(partial_value, (2, 0, 1))
    partial_value = jnp.concatenate(
        [partial_value, jnp.full((1, DOC_DEV, rows), -1000000000.0, jnp.float32)], axis=0
    )
    slotted = jnp.take(partial_value, source, axis=0).reshape(owner_count, capacity, DOC_DEV, rows)
    gathered = jnp.max(slotted, axis=1)
    received = lax.all_to_all(gathered, "wide", split_axis=0, concat_axis=0, tiled=True)
    highest = jnp.max(received, axis=0)
    return finish(highest)


def solution(mesh):
    placed = (
        P(("groups", "wide"), None, None),
        P(("groups", "wide"), None),
        P(("groups", "wide"), None),
        P(("groups", "wide"), None),
        P(),
        P(("groups", "wide"), None),
    )
    return jax.shard_map(
        local, mesh=mesh, in_specs=placed, out_specs=P(("groups", "wide"), None), check_vma=False
    )
```

profile of v0, /device:TPU:0, one launch (start us, length us, event | category | flops | bytes accessed | tf_op | source)
XLA Modules:
  0.0 88.2 jit_solution(5283498672096399284)
XLA Ops:
  0.0 0.0 copy-start
  0.0 0.8 fusion.2
  0.8 0.1 reduce_window_sum.11
  0.9 0.8 select_reduce_fusion.10
  1.7 0.7 iota_add_fusion
  2.4 0.1 select_reduce_fusion.9
  2.5 0.8 broadcast_compare_fusion.6
  3.3 0.0 copy-done
  3.3 0.0 copy-start.1
  3.4 6.3 %multiply_reduce_fusion = (f32[4096]{0:T(1024)S(1)}, f32[4096,128]{0,1:T(8,128)S(1)}) fusion(bf16[4096,1024]{1,0:T(8,128)(2,1)} %bitcast.40, bf16[1024,128]{1,0:T(8,128)(2,1)S(1)} %copy-done), kind=kOutput, calls=%fused_computation.11 | convolution fusion | flops 1074786304 | bytes 10764288 | tf_op jit(solution)/shard_map/dot_general | solution.py:36
  9.7 0.0 copy-done.1
  9.7 23.8 %all_gather.3 = bf16[1024,128]{1,0:T(8,128)(2,1)S(1)} all-gather(bf16[64,128]{1,0:T(8,128)(2,1)S(1)} %copy-done.1), channel_id=1, replica_groups=mesh['groups'=2,'wide'=16] {'wide'}, dimensions={0}, use_global_device_ids=true | all-gather | bytes 278528 | tf_op jit(solution)/shard_map/all_gather | solution.py:46
  33.5 23.4 %select_reduce_fusion = (f32[1024,64]{0,1:T(8,128)S(1)}, f32[1024,64]{0,1:T(8,128)S(1)}, f32[1024,64]{0,1:T(8,128)S(1)}, f32[1024,64]{0,1:T(8,128)S(1)}, f32[102...) fusion(pred[64,64]{1,0:T(8,128)(4,1)S(1)} %get-tuple-element.21, ...), kind=kOutput, calls=%fused_computation.1 | convolution fusion | flops 1141374976 | bytes 4505600 | tf_op jit(solution)/shard_map/dot_general | solution.py:48
  56.9 0.2 stack.27
  57.1 0.2 stack.28
  57.3 0.2 stack.29
  57.5 0.2 stack.30
  57.7 0.2 stack.31
  57.8 0.2 stack.32
  58.0 0.2 stack.33
  58.2 0.2 stack.34
  58.4 0.1 sub.13
  58.5 4.7 %stack.35 = f32[8,1024,64]{1,0,2:T(8,128)} concatenate(f32[1,1024,64]{1,0,2:T(1,128)S(1)} %stack.27, f32[1,1024,64]{1,0,2:T(1,128)S(1)} %stack.28, f32[1,1024,64]{1,0,2:T(1,128)S(1)} %stack.29, f32[1,1024,64]{1,0,2:T(1,128)S(1)} %stack.30, f32[1,1024,64]{1,0,2:T(1,128)S(1)} %stack.31, f32[1,1024,64]{1,0,2:T(1,128)S(1)} %stack.32, f32[1,1024,64]{1,0,2:T(1,128)S(1)} %stack.33, ...), dimensions={0} | concatenate | bytes 4194304 | tf_op jit(solution)/shard_map/stack | solution.py:51
  63.3 1.7 %concatenate.3 = f32[65,8,1024]{2,1,0:T(8,128)S(1)} pad(f32[64,8,1024]{2,1,0:T(8,128)} %bitcast.41, f32[]{:T(128)} %constant.26.clone.1), padding=0_1x0_0x0_0 | pad | bytes 4227076 | tf_op jit(solution)/shard_map/concatenate | solution.py:58
  65.0 2.7 %gather_fusion = f32[128,8,1024]{2,1,0:T(8,128)} fusion(f32[65,8,1024]{2,1,0:T(8,128)S(1)} %concatenate.3, s32[1024]{0:T(1024)S(1)} %pad_clamp_fusion), kind=kCustom, calls=%fused_computation | custom fusion | bytes 8389120 | tf_op jit(solution)/shard_map/jit(_take)/gather | solution.py:61
  67.7 2.9 %select_reduce_fusion.8 = f32[16,8,1024]{2,1,0:T(8,128)S(1)} fusion(pred[16,8]{1,0:T(8,128)(4,1)S(1)} %compare_and_fusion, f32[128,8,1024]{2,1,0:T(8,128)} %gather_fusion), kind=kLoop, calls=%fused_computation.9 | loop fusion | flops 1966080 | bytes 4718720 | tf_op jit(solution)/shard_map/reduce_max | solution.py:62
  70.7 16.9 %all_to_all.5 = f32[16,8,1024]{2,1,0:T(8,128)S(1)} all-to-all(f32[16,8,1024]{2,1,0:T(8,128)S(1)} %select_reduce_fusion.8), channel_id=1, replica_groups=mesh['groups'=2,'wide'=16] {'wide'}, dimensions={0} | all-to-all | bytes 1048576 | tf_op jit(solution)/shard_map/all_to_all | solution.py:63
  87.6 0.6 compare_select_fusion
  (7 shorter events, 0.1 us)
Async XLA Ops:
  0.0 3.3 %copy-start = (bf16[1024,128]{1,0:T(8,128)(2,1)S(1)}, bf16[1024,128]{1,0:T(8,128)(2,1)}, u32[]{:S(2)}) copy-start(bf16[1024,128]{1,0:T(8,128)(2,1)} %param.10) | copy-start | bytes 786436
  3.3 6.3 %copy-start.1 = (bf16[64,128]{1,0:T(8,128)(2,1)S(1)}, bf16[64,128]{1,0:T(8,128)(2,1)}, u32[]{:S(2)}) copy-start(bf16[64,128]{1,0:T(8,128)(2,1)} %param.11) | copy-start | bytes 49156
where the time goes:
time: 88.6 us; the launch traced here: 88.2 us
  blocking collectives  40.7 us (46%)
  matrix products  29.7 us (34%)
  local copies, waits for them, and re-layouts  10.7 us (12%)
  other arithmetic  6.92 us (8%)
    all_gather x1, blocking collectives, local(): query_piece = lax.all_gather(queries, 'wide', axis=0, tiled=True)  23.8 us
    dot_general x1, matrix products, local(): jnp.dot(query_piece, vectors.T, preferred_element_type=jnp.float32)  23.4 us
    all_to_all x1, blocking collectives, local(): lax.all_to_all(gathered, 'wide', split_axis=0, concat_axis=0, tiled=True)  16.9 us
    dot_general x1, matrix products, local(): jnp.dot(hidden_states.reshape(nblocks * block_len, model_width), proj_wei...  6.29 us
    another operation x9, local copies, waits for them, and re-layouts, local(): jnp.stack([jnp.max(jnp.where(doc_code[None, :, :] == doc_slot, similar, -...  6.17 us
    reduce_max x1, other arithmetic, local(): gathered = jnp.max(slotted, axis=1)  2.93 us
    gather x1, local copies, waits for them, and re-layouts, local(): jnp.take(partial_value, source, axis=0)  2.74 us

commit v1 on v0

--- a/solution.py
+++ b/solution.py
@@ -43,7 +43,15 @@
     ).astype(jnp.bfloat16)
     doc_code = jnp.where(token_live == 1, token_doc, -1)
     source = slot_sources(block_owner, owner_count, capacity)
-    query_piece = lax.all_gather(queries, "wide", axis=0, tiled=True)
+    ways, here, step = (lax.axis_size("wide"), lax.axis_index("wide"), queries.shape[0])
+    line, have = (queries, 1)
+    while have < ways:
+        line = jnp.concatenate(
+            [line, lax.ppermute(line, "wide", [(d, (d - have) % ways) for d in range(ways)])],
+            axis=0,
+        )
+        have = 2 * have
+    query_piece = jnp.roll(line, here * step, axis=0)
     rows = query_piece.shape[0]
     similar = jnp.dot(query_piece, vectors.T, preferred_element_type=jnp.float32).reshape(
         rows, nblocks, block_len

time: 88.6 us -> 85.9 us (0.970)
  blocking collectives: 40.7 us -> 19.5 us
  waiting for transfers between devices: 0 us -> 14.3 us
  starting transfers between devices: 0 us -> 6.66 us
  matrix products: 29.7 us -> 27.1 us
    all_gather x1 -> x0, blocking collectives: 23.8 us -> none  [local(): query_piece = lax.all_gather(queries, 'wide', axis=0, tiled=True)]
    ppermute x0 -> x4, waiting for transfers between devices: none -> 14.3 us  [local(): lax.ppermute(line, 'wide', [(d, (d - have) % ways) for d in range(ways)])]
    ppermute x0 -> x4, starting transfers between devices: none -> 6.66 us  [local(): lax.ppermute(line, 'wide', [(d, (d - have) % ways) for d in range(ways)])]
    all_to_all x1, blocking collectives: 16.9 us -> 19.5 us  [local(): lax.all_to_all(gathered, 'wide', split_axis=0, concat_axis=0, tiled=True)]
    dot_general x1, matrix products: 23.4 us -> 20.8 us  [local(): jnp.dot(query_piece, vectors.T, preferred_element_type=jnp.float32)]
  transfers between devices with their start and end apart: 0 -> 4, of which waited for: 0 -> 3; matrix products, arithmetic and copies ran while one was open for 0% -> 11% of each run, Pallas kernels for 0% -> 0%
where the time goes in v1:
time: 85.9 us; the launch traced here: 85.6 us
  matrix products  27.1 us (32%)
  blocking collectives  19.5 us (23%)
  waiting for transfers between devices  14.3 us (17%)
  local copies, waits for them, and re-layouts  10.9 us (13%)
  other arithmetic  6.89 us (8%)
  starting transfers between devices  6.66 us (8%)
    dot_general x1, matrix products, local(): jnp.dot(query_piece, vectors.T, preferred_element_type=jnp.float32)  20.8 us
    all_to_all x1, blocking collectives, local(): lax.all_to_all(gathered, 'wide', split_axis=0, concat_axis=0, tiled=True)  19.5 us
    ppermute x4, waiting for transfers between devices, local(): lax.ppermute(line, 'wide', [(d, (d - have) % ways) for d in range(ways)])  14.3 us
    ppermute x4, starting transfers between devices, local(): lax.ppermute(line, 'wide', [(d, (d - have) % ways) for d in range(ways)])  6.66 us
    dot_general x1, matrix products, local(): jnp.dot(hidden_states.reshape(nblocks * block_len, model_width), proj_wei...  6.28 us
    another operation x9, local copies, waits for them, and re-layouts, local(): jnp.stack([jnp.max(jnp.where(doc_code[None, :, :] == doc_slot, similar, -...  6.17 us
    reduce_max x1, other arithmetic, local(): gathered = jnp.max(slotted, axis=1)  2.93 us
    gather x1, local copies, waits for them, and re-layouts, local(): jnp.take(partial_value, source, axis=0)  2.74 us
  transfers between devices with their start and end apart: 4, of which 3 were waited for; matrix products, arithmetic and copies ran while one was open for 11% of the time, Pallas kernels for 0%

profile of v1, /device:TPU:0, one launch (start us, length us, event | category | flops | bytes accessed | tf_op | source)
XLA Modules:
  0.0 85.6 jit_solution(6150466318610067144)
XLA Ops:
  0.0 0.0 copy-start
  0.0 5.5 %collective-permute-start = (bf16[64,128]{1,0:T(8,128)(2,1)}, bf16[64,128]{1,0:T(8,128)(2,1)S(1)}, u32[]{:S(2)}, u32[]{:S(2)}) collective-permute-start(bf16[64,128]{1,0:T(8,128)(2,1)} %param.11), channel_id=1, source_target_pairs={{0,15},{1,0},{2,1},{3,2},{4,3},{5,4},{6,5},{7,6},{8,7},{9,8},{10,9... | collective-permute-start | bytes 49160 | tf_op jit(solution)/shard_map/ppermute | solution.py:50
  5.5 0.7 fusion.3
  6.2 0.1 reduce_window_sum.11
  6.3 0.8 select_reduce_fusion.10
  7.1 0.7 iota_add_fusion
  7.8 0.1 select_reduce_fusion.9
  7.9 0.8 broadcast_compare_fusion.6
  8.8 0.0 copy-done
  8.8 0.0 copy-start.1
  8.8 6.3 %multiply_reduce_fusion = (f32[4096]{0:T(1024)S(1)}, f32[4096,128]{0,1:T(8,128)S(1)}) fusion(bf16[4096,1024]{1,0:T(8,128)(2,1)} %bitcast.37, bf16[1024,128]{1,0:T(8,128)(2,1)S(1)} %copy-done), kind=kOutput, calls=%fused_computation.11 | convolution fusion | flops 1074786304 | bytes 10764288 | tf_op jit(solution)/shard_map/dot_general | solution.py:36
  15.1 0.1 sub.17
  15.2 0.0 copy-done.1
  15.2 0.0 collective-permute-done
  15.2 0.7 collective-permute-start.1
  15.9 3.3 %collective-permute-done.1 = bf16[128,128]{1,0:T(8,128)(2,1)S(1)} collective-permute-done((bf16[128,128]{1,0:T(8,128)(2,1)S(1)}, bf16[128,128]{1,0:T(8,128)(2,1)S(1)}, u32[]{:S(2)}, u32[]{:S(2)}) %collective-permute-start.1) | collective-permute-done | bytes 32800 | tf_op jit(solution)/shard_map/ppermute | solution.py:50
  19.2 0.5 collective-permute-start.2
  19.7 3.8 %collective-permute-done.2 = bf16[256,128]{1,0:T(8,128)(2,1)S(1)} collective-permute-done((bf16[256,128]{1,0:T(8,128)(2,1)S(1)}, bf16[256,128]{1,0:T(8,128)(2,1)S(1)}, u32[]{:S(2)}, u32[]{:S(2)}) %collective-permute-start.2) | collective-permute-done | bytes 65568 | tf_op jit(solution)/shard_map/ppermute | solution.py:50
  23.5 0.1 collective-permute-start.3
  23.6 7.2 %collective-permute-done.3 = bf16[512,128]{1,0:T(8,128)(2,1)S(1)} collective-permute-done((bf16[512,128]{1,0:T(8,128)(2,1)S(1)}, bf16[512,128]{1,0:T(8,128)(2,1)S(1)}, u32[]{:S(2)}, u32[]{:S(2)}) %collective-permute-start.3) | collective-permute-done | bytes 131104 | tf_op jit(solution)/shard_map/ppermute | solution.py:50
  30.9 20.8 %select_reduce_fusion = (f32[1024,64]{0,1:T(8,128)S(1)}, f32[1024,64]{0,1:T(8,128)S(1)}, f32[1024,64]{0,1:T(8,128)S(1)}, f32[1024,64]{0,1:T(8,128)S(1)}, f32[102...) fusion(pred[64,64]{1,0:T(8,128)(4,1)S(1)} %get-tuple-element.21, ...), kind=kOutput, calls=%fused_computation.1 | convolution fusion | flops 1141374976 | bytes 4538372 | tf_op jit(solution)/shard_map/dot_general | solution.py:56
  51.8 0.2 stack.27
  52.0 0.2 stack.28
  52.1 0.2 stack.29
  52.3 0.2 stack.30
  52.5 0.2 stack.31
  52.7 0.2 stack.32
  52.9 0.2 stack.33
  53.1 0.2 stack.34
  53.3 4.7 %stack.35 = f32[8,1024,64]{1,0,2:T(8,128)} concatenate(f32[1,1024,64]{1,0,2:T(1,128)S(1)} %stack.27, f32[1,1024,64]{1,0,2:T(1,128)S(1)} %stack.28, f32[1,1024,64]{1,0,2:T(1,128)S(1)} %stack.29, f32[1,1024,64]{1,0,2:T(1,128)S(1)} %stack.30, f32[1,1024,64]{1,0,2:T(1,128)S(1)} %stack.31, f32[1,1024,64]{1,0,2:T(1,128)S(1)} %stack.32, f32[1,1024,64]{1,0,2:T(1,128)S(1)} %stack.33, ...), dimensions={0} | concatenate | bytes 4194304 | tf_op jit(solution)/shard_map/stack | solution.py:59
  58.0 1.7 %concatenate.25 = f32[65,8,1024]{2,1,0:T(8,128)S(1)} pad(f32[64,8,1024]{2,1,0:T(8,128)} %bitcast.38, f32[]{:T(128)} %constant.73.clone.1), padding=0_1x0_0x0_0 | pad | bytes 4227076 | tf_op jit(solution)/shard_map/concatenate | solution.py:66
  59.7 2.7 %gather_fusion = f32[128,8,1024]{2,1,0:T(8,128)} fusion(f32[65,8,1024]{2,1,0:T(8,128)S(1)} %concatenate.25, s32[1024]{0:T(1024)S(1)} %pad_clamp_fusion), kind=kCustom, calls=%fused_computation | custom fusion | bytes 8389120 | tf_op jit(solution)/shard_map/jit(_take)/gather | solution.py:69
  62.5 2.9 %select_reduce_fusion.8 = f32[16,8,1024]{2,1,0:T(8,128)S(1)} fusion(pred[16,8]{1,0:T(8,128)(4,1)S(1)} %compare_and_fusion, f32[128,8,1024]{2,1,0:T(8,128)} %gather_fusion), kind=kLoop, calls=%fused_computation.9 | loop fusion | flops 1966080 | bytes 4718720 | tf_op jit(solution)/shard_map/reduce_max | solution.py:70
  65.4 19.5 %all_to_all.5 = f32[16,8,1024]{2,1,0:T(8,128)S(1)} all-to-all(f32[16,8,1024]{2,1,0:T(8,128)S(1)} %select_reduce_fusion.8), channel_id=1, replica_groups=mesh['groups'=2,'wide'=16] {'wide'}, dimensions={0} | all-to-all | bytes 1048576 | tf_op jit(solution)/shard_map/all_to_all | solution.py:71
  85.0 0.6 compare_select_fusion
  (20 shorter events, 0.2 us)
Async XLA Ops:
  0.0 8.8 %copy-start = (bf16[1024,128]{1,0:T(8,128)(2,1)S(1)}, bf16[1024,128]{1,0:T(8,128)(2,1)}, u32[]{:S(2)}) copy-start(bf16[1024,128]{1,0:T(8,128)(2,1)} %param.10) | copy-start | bytes 786436
  0.0 15.2 %collective-permute-start = (bf16[64,128]{1,0:T(8,128)(2,1)}, bf16[64,128]{1,0:T(8,128)(2,1)S(1)}, u32[]{:S(2)}, u32[]{:S(2)}) collective-permute-start(bf16[64,128]{1,0:T(8,128)(2,1)} %param.11), channel_id=1, source_target_pairs={{0,15},{1,0},{2,1},{3,2},{4,3},{5,4},{6,5},{7,6},{8,7},{9,8},{10,9... | collective-permute-start | bytes 49160 | tf_op jit(solution)/shard_map/ppermute | solution.py:50
  8.8 6.4 %copy-start.1 = (bf16[64,128]{1,0:T(8,128)(2,1)S(1)}, bf16[64,128]{1,0:T(8,128)(2,1)}, u32[]{:S(2)}) copy-start(bf16[64,128]{1,0:T(8,128)(2,1)} %param.11) | copy-start | bytes 49156
  15.2 4.0 %collective-permute-start.1 = (bf16[128,128]{1,0:T(8,128)(2,1)S(1)}, bf16[128,128]{1,0:T(8,128)(2,1)S(1)}, u32[]{:S(2)}, u32[]{:S(2)}) collective-permute-start(bf16[128,128]{1,0:T(8,128)(2,1)S(1)} %pad_maximum_fusion.2), channel_id=1, source_target_pairs={{0,14},{1,15},{2,0},{3,1},{4,2},{5,3},{6,4},{7,5},{8,6},{9,7},{10,... | collective-permute-start | bytes 98312 | tf_op jit(solution)/shard_map/ppermute | solution.py:50
  19.2 4.3 %collective-permute-start.2 = (bf16[256,128]{1,0:T(8,128)(2,1)S(1)}, bf16[256,128]{1,0:T(8,128)(2,1)S(1)}, u32[]{:S(2)}, u32[]{:S(2)}) collective-permute-start(bf16[256,128]{1,0:T(8,128)(2,1)S(1)} %pad_maximum_fusion.1), channel_id=1, source_target_pairs={{0,12},{1,13},{2,14},{3,15},{4,0},{5,1},{6,2},{7,3},{8,4},{9,5},{1... | collective-permute-start | bytes 196616 | tf_op jit(solution)/shard_map/ppermute | solution.py:50
  23.5 7.3 %collective-permute-start.3 = (bf16[512,128]{1,0:T(8,128)(2,1)S(1)}, bf16[512,128]{1,0:T(8,128)(2,1)S(1)}, u32[]{:S(2)}, u32[]{:S(2)}) collective-permute-start(bf16[512,128]{1,0:T(8,128)(2,1)S(1)} %pad_maximum_fusion), channel_id=1, source_target_pairs={{0,8},{1,9},{2,10},{3,11},{4,12},{5,13},{6,14},{7,15},{8,0},{9,1},... | collective-permute-start | bytes 393224 | tf_op jit(solution)/shard_map/ppermute | solution.py:50
